TPU v7x, 32 devices: a whole 2x2x4 slice. The times are simulated.
32 devices in a mesh: groups: 2 (over x), blk: 16 (over z, y, core).
Axes of the slice: x: 2, y: 2, z: 4, core: 2. Of those that a mesh axis runs over, the one named last changes fastest.
Arguments:
- hidden: bfloat16 [32, 512, 640], P(('groups', 'blk')), parts along dimension 0, may hold values from -6 to 6
- query_weight: bfloat16 [16, 2560, 640], P('blk')
- query_gain: float32 [5120], replicated, may hold values from 0.1 to 32
- frame_cache: bfloat16 [32, 2, 8, 2, 16, 640], P(('groups', 'blk')), parts along dimension 0, may hold values from -8.1 to 8.1
- span_kv: bfloat16 [32, 2, 512, 640], P(('groups', 'blk')), parts along dimension 0, may hold values from -8 to 8
- selected: int32 [4, 12], P('groups'), parts along dimension 0, may hold values from 1 to 13, as said below
- owner: int32 [4, 16], P('groups'), parts along dimension 0, may hold values from 0 to 15, each once within a row
Outputs:
- attended: bfloat16 [32, 512, 640], P(('groups', 'blk')), parts along dimension 0
There are 2 independent parts, one for each index of `groups`. A program takes and returns all parts, laid end to end along the dimension named above; an argument that names none is the same for every part. Nothing has to cross between parts.
Inputs may be any that keep to these rules, and one draw needn't show every extreme that they name: `selected`: each row names 12 different frames strictly between the first frame and the last 2; frame 16 - 3 is always among them. Each row of owner names every device of the part once, so a device keeps one frame of every rollout.
All inputs are finite; a program needn't handle non-finite values.
Results may differ from a plain program's by a relative error of at most 0.012.
The roundings to bfloat16 on the way count: a program that leaves them out, or rounds other values in their place, can miss the bound.
Values may be sent and summed in bfloat16 or wider, within the bound.
A program may use at most 64 MiB of HBM per device.

v0:
```python
import jax
import jax.numpy as jnp
from jax import lax
from jax.sharding import PartitionSpec as P

HD = 128
HG = 8
norm_epsilon = 1e-06


def from_partner(block, axis, distance):
    count = lax.axis_size(axis)
    route = []
    for low in range(count):
        high = low | 1 << distance
        if high != low and high < count:
            route += [(low, high), (high, low)]
    return lax.ppermute(block, axis, route)


def passed_along(array, axis, by):
    length = lax.axis_size(axis)
    return lax.ppermute(array, axis, [(i, (i + by) % length) for i in range(length)])


def add_columns(running, features, block_piece, offset):
    columns = lax.dynamic_slice_in_dim(features, offset, block_piece.shape[0], 1)
    return running + jnp.dot(columns, block_piece, preferred_element_type=jnp.float32)


def shards(hidden, query_weight, query_gain, frame_cache, span_kv, selected, owner):
    device = lax.axis_index("blk")
    device_count = lax.axis_size("blk")
    slot_count = device_count // HG
    slot_index = device // HG
    group_index = device % HG
    group_width = hidden.shape[2]
    bit_count = HG.bit_length() - 1
    features = hidden[0]
    for bit_number in range(bit_count):
        partner = from_partner(features, "blk", bit_number)
        upper_half = (group_index >> bit_number) % 2 == 1
        features = jnp.where(
            upper_half,
            jnp.concatenate([partner, features], 1),
            jnp.concatenate([features, partner], 1),
        )
    own_block = query_weight[0]
    block_rows = own_block.shape[0]
    running = jnp.zeros((features.shape[0], group_width), jnp.float32)
    half_rows = block_rows // 2
    first_half = own_block[:half_rows]
    second_half = own_block[half_rows:]
    running = add_columns(running, features, first_half, slot_index * block_rows)
    running = add_columns(running, features, second_half, slot_index * block_rows + half_rows)

    def turn_both(turn_index, loop_state):
        partial_sum, leading, trailing = loop_state
        leading = passed_along(leading, "blk", HG)
        trailing = passed_along(trailing, "blk", -HG)
        earlier = (slot_index - turn_index) % slot_count
        later = (slot_index + turn_index) % slot_count
        partial_sum = add_columns(partial_sum, features, leading, earlier * block_rows)
        partial_sum = add_columns(partial_sum, features, trailing, later * block_rows + half_rows)
        return (partial_sum, leading, trailing)

    running, _, _ = lax.fori_loop(1, slot_count, turn_both, (running, first_half, second_half))
    energy = jnp.sum(running * running, axis=1)
    for bit_number in range(bit_count):
        energy = energy + from_partner(energy, "blk", bit_number)
    row_scale = lax.rsqrt(energy / features.shape[1] + norm_epsilon)
    gain_slice = lax.dynamic_slice_in_dim(query_gain, group_index * group_width, group_width)
    query_rows = (running * row_scale[:, None] * gain_slice).astype(jnp.bfloat16)
    outgoing = frame_cache[0]
    outgoing = outgoing.reshape((-1,) + outgoing.shape[2:])
    incoming = lax.all_to_all(outgoing, "blk", split_axis=0, concat_axis=0, tiled=True)
    frame_count = owner.shape[1]
    window_frames = frame_count // 8
    frame_time = jnp.arange(frame_count, dtype=jnp.int32)
    chosen = (
        (frame_time == 0)
        | (frame_time >= frame_count - window_frames)
        | jnp.any(frame_time[:, None] == selected[slot_index][None, :], axis=1)
    )
    placed = owner[slot_index][:, None] == jnp.arange(device_count, dtype=jnp.int32)[None, :]
    owner_kept = jnp.any(placed & chosen[:, None], axis=0)
    frame_tokens = incoming.shape[2]
    key_rows = jnp.concatenate([incoming[:, 0].reshape(-1, group_width), span_kv[0, 0]], 0)
    value_rows = jnp.concatenate([incoming[:, 1].reshape(-1, group_width), span_kv[0, 1]], 0)
    visible = jnp.concatenate(
        [jnp.repeat(owner_kept, frame_tokens), jnp.ones((query_rows.shape[0],), dtype=bool)]
    )
    head_count = group_width // HD

    def one_head(head_index):
        start = head_index * HD
        query_part = lax.dynamic_slice_in_dim(query_rows, start, HD, 1)
        key_part = lax.dynamic_slice_in_dim(key_rows, start, HD, 1)
        value_part = lax.dynamic_slice_in_dim(value_rows, start, HD, 1)
        scores = lax.dot_general(
            query_part, key_part, (((1,), (1,)), ((), ())), preferred_element_type=jnp.float32
        ) * HD ** (-0.5)
        highest = jnp.max(jnp.where(visible, scores, -jnp.inf), axis=1, keepdims=True)
        probs = jnp.where(visible, jnp.exp(scores - highest), 0.0)
        totals = jnp.sum(probs, axis=1, keepdims=True)
        mixed_rows = jnp.dot(
            probs.astype(jnp.bfloat16), value_part, preferred_element_type=jnp.float32
        )
        return (mixed_rows / totals).astype(jnp.bfloat16)

    head_outputs = lax.map(one_head, jnp.arange(head_count, dtype=jnp.int32))
    return jnp.transpose(head_outputs, (1, 0, 2)).reshape(1, query_rows.shape[0], group_width)


def solution(mesh):
    in_specs = (
        P(("groups", "blk"), None, None),
        P("blk", None, None),
        P(),
        P(("groups", "blk"), None, None, None, None, None),
        P(("groups", "blk"), None, None, None),
        P("groups", None),
        P("groups", None),
    )
    out_specs = P(("groups", "blk"), None, None)
    return jax.shard_map(shards, mesh=mesh, in_specs=in_specs, out_specs=out_specs, check_vma=False)
```

profile of v0, /device:TPU:0, one launch (start us, length us, event | category | flops | bytes accessed | tf_op | source)
XLA Modules:
  0.0 231.8 jit_solution(16575466345846282832)
XLA Ops:
  0.5 1.9 collective-permute-done
  2.4 1.7 maximum_select_fusion.2
  4.1 3.0 %collective-permute-start.1 = (bf16[512,1280]{1,0:T(8,128)(2,1)S(1)}, bf16[512,1280]{1,0:T(8,128)(2,1)}, u32[]{:S(2)}, u32[]{:S(2)}) collective-permute-start(bf16[512,1280]{1,0:T(8,128)(2,1)S(1)} %maximum_select_fusion.2), channel_id=1, source_target_pairs={{0,2},{2,0},{1,3},{3,1},{4,6},{6,4},{5,7},{7,5},{8,10},{10,8},{9,1... | collective-permute-start | bytes 3932168 | tf_op jit(solution)/shard_map/ppermute | solution.py:18
  7.0 29.2 %collective-permute-done.1 = bf16[512,1280]{1,0:T(8,128)(2,1)} collective-permute-done((bf16[512,1280]{1,0:T(8,128)(2,1)S(1)}, bf16[512,1280]{1,0:T(8,128)(2,1)}, u32[]{:S(2)}, u32[]{:S(2)}) %collective-permute-start.1) | collective-permute-done | bytes 1310752 | tf_op jit(solution)/shard_map/ppermute | solution.py:18
  36.2 3.0 %maximum_select_fusion.1 = bf16[512,2560]{1,0:T(8,128)(2,1)S(1)} fusion(bf16[512,1280]{1,0:T(8,128)(2,1)} %copy-done.3, bf16[512,1280]{1,0:T(8,128)(2,1)} %collective-permute-done.1, pred[]{:T(512)S(6)} %eq.64), kind=kLoop, calls=%fused_computation.19 | loop fusion | flops 11796480 | bytes 5242881 | tf_op jit(solution)/shard_map/jit(_where)/select_n | solution.py:43
  39.2 1.9 collective-permute-start.2
  41.1 2.0 slice_bitcast_fusion.1
  43.1 2.6 %collective-permute-start.3 = (bf16[1280,640]{1,0:T(8,128)(2,1)}, bf16[1280,640]{1,0:T(8,128)(2,1)}, u32[]{:S(2)}, u32[]{:S(2)}) collective-permute-start(bf16[1280,640]{1,0:T(8,128)(2,1)} %get-tuple-element.80), channel_id=1, source_target_pairs={{0,8},{1,9},{2,10},{3,11},{4,12},{5,13},{6,14},{7,15},{8,0},{9,1},... | collective-permute-start | bytes 4915208 | tf_op jit(solution)/shard_map/while/body/eval_jaxpr/ppermute | solution.py:23
  46.0 4.9 %all-to-all-start = ((bf16[16,2,16,640]{3,2,1,0:T(8,128)(2,1)}), bf16[16,2,16,640]{3,2,1,0:T(8,128)(2,1)S(1)}, u32[]{:S(2)}, u32[]{:S(2)}) async-start(bf16[16,2,16,640]{3,2,1,0:T(8,128)(2,1)} %bitcast.34), calls=%async_computation | async-start | bytes 1310720 | tf_op jit(solution)/shard_map/all_to_all | solution.py:76
  51.2 2.5 %slice_bitcast_fusion.2 = (bf16[512,640]{1,0:T(8,128)(2,1)}, bf16[512,640]{1,0:T(8,128)(2,1)}) fusion(bf16[1,2,512,640]{3,2,1,0:T(8,128)(2,1)} %param.13), kind=kLoop, calls=%fused_computation.37 | loop fusion | bytes 2621440 | tf_op jit(solution)/shard_map/squeeze | solution.py:89
  53.7 99.3 %collective-permute-done.2 = bf16[512,2560]{1,0:T(8,128)(2,1)} collective-permute-done((bf16[512,2560]{1,0:T(8,128)(2,1)S(1)}, bf16[512,2560]{1,0:T(8,128)(2,1)}, u32[]{:S(2)}, u32[]{:S(2)}) %collective-permute-start.2) | collective-permute-done | bytes 2621472 | tf_op jit(solution)/shard_map/ppermute | solution.py:18
  153.0 4.5 %maximum_select_fusion = bf16[512,5120]{1,0:T(8,128)(2,1)S(1)} fusion(bf16[512,2560]{1,0:T(8,128)(2,1)S(1)} %maximum_select_fusion.1, bf16[512,2560]{1,0:T(8,128)(2,1)} %collective-permute-done.2, pred[]{:T(512)S(6)} %eq.63), kind=kLoop, calls=%fused_computation.18 | loop fusion | flops 23592960 | bytes 10485761 | tf_op jit(solution)/shard_map/jit(_where)/select_n | solution.py:43
  157.6 1.2 fusion.20
  158.8 2.7 %fusion.18 = f32[512,640]{1,0:T(8,128)S(1)} fusion(bf16[1280,640]{1,0:T(8,128)(2,1)} %collective-permute-done.3, bf16[512,5120]{1,0:T(8,128)(2,1)S(1)} %maximum_select_fusion, s32[]{:T(128)S(6)} %select_n.106), kind=kOutput, calls=%fused_computation.30 | convolution fusion | flops 838860800 | bytes 4259844 | tf_op jit(solution)/shard_map/while/body/eval_jaxpr/dot_general | solution.py:28
  161.4 33.9 %collective-permute-done.4 = bf16[1280,640]{1,0:T(8,128)(2,1)} collective-permute-done((bf16[1280,640]{1,0:T(8,128)(2,1)}, bf16[1280,640]{1,0:T(8,128)(2,1)}, u32[]{:S(2)}, u32[]{:S(2)}) %collective-permute-start.4) | collective-permute-done | bytes 1638432 | tf_op jit(solution)/shard_map/while/body/eval_jaxpr/ppermute | solution.py:23
  195.4 2.6 %fusion.16 = f32[512,640]{1,0:T(8,128)S(1)} fusion(bf16[1280,640]{1,0:T(8,128)(2,1)} %collective-permute-done.4, bf16[512,5120]{1,0:T(8,128)(2,1)S(1)} %maximum_select_fusion, s32[]{:T(128)S(6)} %select_n.108), kind=kOutput, calls=%fused_computation.28 | convolution fusion | flops 838860800 | bytes 4259844 | tf_op jit(solution)/shard_map/while/body/eval_jaxpr/dot_general | solution.py:28
  198.0 1.3 multiply_reduce_fusion
  199.7 0.8 dynamic_slice.42
  200.5 1.5 collective-permute-start.6
  202.1 2.0 collective-permute-done.6
  204.1 2.3 pad_maximum_fusion
  206.4 1.3 collective-permute-done.7
  207.9 21.7 %while.2 = (s32[]{:T(128)}, bf16[5,512,128]{1,2,0:T(8,128)(2,1)}, pred[768]{0:T(1024)(128)(4,1)S(1)}, s32[5]{0:T(128)S(1)}, bf16[512,640]{1,0:T(8,128)(2,1)S(1)}...) while((s32[]{:T(128)}, bf16[5,512,128]{1,2,0:T(8,128)(2,1)}, ...), condition=%wide.region_6.7_spmd, body=%wide.region_3.6_spmd.sunk | while | flops 204995584 | bytes 5912747 | solution.py:111
  210.1 1.4 fusion.42
  211.6 0.7 constant_dynamic-update-slice_fusion.2
  214.4 1.4 fusion.42
  218.8 1.4 fusion.42
  220.3 0.7 constant_dynamic-update-slice_fusion.2
  223.1 1.4 fusion.42
  227.5 1.4 fusion.42
  229.0 0.7 constant_dynamic-update-slice_fusion.2
  229.7 2.2 copy.16
  (56 shorter events, 10.9 us)
Async XLA Ops:
  0.0 51.2 %copy-start = (s32[2,16]{1,0:T(2,128)S(1)}, s32[2,16]{1,0:T(2,128)}, u32[]{:S(2)}) copy-start(s32[2,16]{1,0:T(2,128)} %param.15) | copy-start | bytes 388
  0.0 2.4 %collective-permute-start = (bf16[512,640]{1,0:T(8,128)(2,1)}, bf16[512,640]{1,0:T(8,128)(2,1)S(1)}, u32[]{:S(2)}, u32[]{:S(2)}) collective-permute-start(bf16[512,640]{1,0:T(8,128)(2,1)} %bitcast.36), channel_id=1, source_target_pairs={{0,1},{1,0},{2,3},{3,2},{4,5},{5,4},{6,7},{7,6},{8,9},{9,8},{10,11... | collective-permute-start | bytes 1966088 | tf_op jit(solution)/shard_map/ppermute | solution.py:18
  4.1 3.0 %copy-start.3 = (bf16[512,1280]{1,0:T(8,128)(2,1)}, bf16[512,1280]{1,0:T(8,128)(2,1)S(1)}, u32[]{:S(2)}) copy-start(bf16[512,1280]{1,0:T(8,128)(2,1)S(1)} %maximum_select_fusion.2) | copy-start | bytes 3932164
  4.1 32.1 %collective-permute-start.1 = (bf16[512,1280]{1,0:T(8,128)(2,1)S(1)}, bf16[512,1280]{1,0:T(8,128)(2,1)}, u32[]{:S(2)}, u32[]{:S(2)}) collective-permute-start(bf16[512,1280]{1,0:T(8,128)(2,1)S(1)} %maximum_select_fusion.2), channel_id=1, source_target_pairs={{0,2},{2,0},{1,3},{3,1},{4,6},{6,4},{5,7},{7,5},{8,10},{10,8},{9,1... | collective-permute-start | bytes 3932168 | tf_op jit(solution)/shard_map/ppermute | solution.py:18
  7.0 34.0 %copy-start.1 = (bf16[1,2560,640]{2,1,0:T(8,128)(2,1)S(1)}, bf16[1,2560,640]{2,1,0:T(8,128)(2,1)}, u32[]{:S(2)}) copy-start(bf16[1,2560,640]{2,1,0:T(8,128)(2,1)} %param.10) | copy-start | bytes 9830404
  39.2 11.8 %copy-start.5 = (s32[2,12]{1,0:T(2,128)S(1)}, s32[2,12]{1,0:T(2,128)}, u32[]{:S(2)}) copy-start(s32[2,12]{1,0:T(2,128)} %param.14) | copy-start | bytes 292
  39.2 113.8 %collective-permute-start.2 = (bf16[512,2560]{1,0:T(8,128)(2,1)S(1)}, bf16[512,2560]{1,0:T(8,128)(2,1)}, u32[]{:S(2)}, u32[]{:S(2)}) collective-permute-start(bf16[512,2560]{1,0:T(8,128)(2,1)S(1)} %maximum_select_fusion.1), channel_id=1, source_target_pairs={{0,4},{4,0},{1,5},{5,1},{2,6},{6,2},{3,7},{7,3},{8,12},{12,8},{9,1... | collective-permute-start | bytes 7864328 | tf_op jit(solution)/shard_map/ppermute | solution.py:18
  43.1 115.7 %collective-permute-start.3 = (bf16[1280,640]{1,0:T(8,128)(2,1)}, bf16[1280,640]{1,0:T(8,128)(2,1)}, u32[]{:S(2)}, u32[]{:S(2)}) collective-permute-start(bf16[1280,640]{1,0:T(8,128)(2,1)} %get-tuple-element.80), channel_id=1, source_target_pairs={{0,8},{1,9},{2,10},{3,11},{4,12},{5,13},{6,14},{7,15},{8,0},{9,1},... | collective-permute-start | bytes 4915208 | tf_op jit(solution)/shard_map/while/body/eval_jaxpr/ppermute | solution.py:23
  45.6 149.7 %collective-permute-start.4 = (bf16[1280,640]{1,0:T(8,128)(2,1)}, bf16[1280,640]{1,0:T(8,128)(2,1)}, u32[]{:S(2)}, u32[]{:S(2)}) collective-permute-start(bf16[1280,640]{1,0:T(8,128)(2,1)} %get-tuple-element.81), channel_id=1, source_target_pairs={{0,8},{1,9},{2,10},{3,11},{4,12},{5,13},{6,14},{7,15},{8,0},{9,1},... | collective-permute-start | bytes 4915208 | tf_op jit(solution)/shard_map/while/body/eval_jaxpr/ppermute | solution.py:23
  46.0 156.1 %all-to-all-start = ((bf16[16,2,16,640]{3,2,1,0:T(8,128)(2,1)}), bf16[16,2,16,640]{3,2,1,0:T(8,128)(2,1)S(1)}, u32[]{:S(2)}, u32[]{:S(2)}) async-start(bf16[16,2,16,640]{3,2,1,0:T(8,128)(2,1)} %bitcast.34), calls=%async_computation | async-start | bytes 1310720 | tf_op jit(solution)/shard_map/all_to_all | solution.py:76
  53.7 103.9 %copy-start.2 = (bf16[1,2560,640]{2,1,0:T(8,128)(2,1)S(1)}, bf16[1,2560,640]{2,1,0:T(8,128)(2,1)}, u32[]{:S(2)}) copy-start(bf16[1,2560,640]{2,1,0:T(8,128)(2,1)} %param.10) | copy-start | bytes 9830404
  199.3 4.8 %copy-start.4 = (bf16[512,640]{1,0:T(8,128)(2,1)S(1)}, bf16[512,640]{1,0:T(8,128)(2,1)}, u32[]{:S(2)}) copy-start(bf16[512,640]{1,0:T(8,128)(2,1)} %get-tuple-element.82) | copy-start | bytes 1966084
  199.3 1.2 collective-permute-start.5
  200.5 3.6 %collective-permute-start.6 = (f32[512]{0:T(512)S(1)}, f32[512]{0:T(512)S(1)}, u32[]{:S(2)}, u32[]{:S(2)}) collective-permute-start(f32[512]{0:T(512)S(1)} %add.114), channel_id=1, source_target_pairs={{0,2},{2,0},{1,3},{3,1},{4,6},{6,4},{5,7},{7,5},{8,10},{10,8},{9,1... | collective-permute-start | bytes 6152 | tf_op jit(solution)/shard_map/ppermute | solution.py:18
  204.1 3.6 %collective-permute-start.7 = (f32[512]{0:T(512)S(1)}, f32[512]{0:T(512)S(1)}, u32[]{:S(2)}, u32[]{:S(2)}) collective-permute-start(f32[512]{0:T(512)S(1)} %add.115), channel_id=1, source_target_pairs={{0,4},{4,0},{1,5},{5,1},{2,6},{6,2},{3,7},{7,3},{8,12},{12,8},{9,1... | collective-permute-start | bytes 6152 | tf_op jit(solution)/shard_map/ppermute | solution.py:18
where the time goes:
time: 232 us
  waiting for transfers between devices  168 us (72%)
  matrix products  17.2 us (7%)
  starting transfers between devices  14.7 us (6%)
  local copies, waits for them, and re-layouts  14.5 us (6%)
  other arithmetic  14.1 us (6%)
  loops' own time  3.36 us (1%)
    ppermute x6, waiting for transfers between devices, from_partner(): return lax.ppermute(block, axis, route)  134 us
    ppermute x2, waiting for transfers between devices, passed_along(): lax.ppermute(array, axis, [(i, (i + by) % length) for i in range(length)])  33.9 us
    select_n x3, other arithmetic, shards(): jnp.where(upper_half, jnp.concatenate([partner, features], 1), jnp.concat...  9.16 us
    dot_general x4, matrix products, add_columns(): jnp.dot(columns, block_piece, preferred_element_type=jnp.float32)  7.81 us
    dot_general x5, matrix products, one_head(): jnp.dot(probs.astype(jnp.bfloat16), value_part, preferred_element_type=jn...  7.09 us
    ppermute x6, starting transfers between devices, from_partner(): return lax.ppermute(block, axis, route)  6.86 us
    all_to_all x1, starting transfers between devices, shards(): lax.all_to_all(outgoing, 'blk', split_axis=0, concat_axis=0, tiled=True)  4.93 us
  transfers between devices with their start and end apart: 9, of which 7 were waited for; matrix products, arithmetic and copies ran while one was open for 9% of the time, Pallas kernels for 0%

commit v1 on v0

--- a/solution.py
+++ b/solution.py
@@ -6,6 +6,33 @@
 HD = 128
 HG = 8
 norm_epsilon = 1e-06
+
+
+def time_group_up(unit, out_dim, piece_in):
+    u_next, o_now = (unit.shape[:out_dim], unit.shape[out_dim + 1 :])
+    latest = jnp.moveaxis(unit.reshape(*u_next, piece_in, -1, *o_now), out_dim, 0)
+    return latest
+
+
+def guide_the_frames(sample, which_dim):
+    sample = jnp.moveaxis(sample, 0, which_dim)
+    oldest = sample.shape
+    x_next = sample.reshape(
+        *oldest[:which_dim], oldest[which_dim] * oldest[which_dim + 1], *oldest[which_dim + 2 :]
+    )
+    return x_next
+
+
+def regions_expand(my_tile, across, matrix, payload):
+    parts_out, top = (jax.lax.axis_size(across), jax.lax.axis_index(across))
+    v1 = time_group_up(payload, matrix, parts_out)
+    entries = [v1[top]]
+    for dev_j in range(1, parts_out):
+        n_now = v1[top ^ dev_j]
+        entries.append(jax.lax.ppermute(n_now, across, [(m, m ^ dev_j) for m in range(parts_out)]))
+    v1 = jnp.stack(entries)[top ^ jnp.arange(parts_out)]
+    tall = guide_the_frames(v1, my_tile)
+    return tall
 
 
 def from_partner(block, axis, distance):
@@ -73,7 +100,7 @@
     query_rows = (running * row_scale[:, None] * gain_slice).astype(jnp.bfloat16)
     outgoing = frame_cache[0]
     outgoing = outgoing.reshape((-1,) + outgoing.shape[2:])
-    incoming = lax.all_to_all(outgoing, "blk", split_axis=0, concat_axis=0, tiled=True)
+    incoming = regions_expand(0, "blk", 0, outgoing)
     frame_count = owner.shape[1]
     window_frames = frame_count // 8
     frame_time = jnp.arange(frame_count, dtype=jnp.int32)

time: 232 us -> 293 us (1.26)
  waiting for transfers between devices: 168 us -> 213 us
  starting transfers between devices: 14.7 us -> 28.2 us
  local copies, waits for them, and re-layouts: 14.5 us -> 27 us
  matrix products: 17.2 us -> 10.7 us
  other arithmetic: 14.1 us -> 10.7 us
    ppermute x6, waiting for transfers between devices: 134 us -> 29.9 us  [from_partner(): return lax.ppermute(block, axis, route)]
    ppermute x2, waiting for transfers between devices: 33.9 us -> 135 us  [passed_along(): lax.ppermute(array, axis, [(i, (i + by) % length) for i in range(length)])]
    ppermute x0 -> x15, waiting for transfers between devices: none -> 47.3 us  [regions_expand(): jax.lax.ppermute(n_now, across, [(m, m ^ dev_j) for m in range(parts_out)])]
    ppermute x0 -> x15, starting transfers between devices: none -> 21.7 us  [regions_expand(): jax.lax.ppermute(n_now, across, [(m, m ^ dev_j) for m in range(parts_out)])]
    unnamed x12 -> x34, local copies, waits for them, and re-layouts: 0.03 us -> 11.7 us
    all_to_all x1 -> x0, starting transfers between devices: 4.93 us -> none  [shards(): lax.all_to_all(outgoing, 'blk', split_axis=0, concat_axis=0, tiled=True)]
    dot_general x5, matrix products: 7.09 us -> 2.48 us  [one_head(): jnp.dot(probs.astype(jnp.bfloat16), value_part, preferred_element_type=jn...]
    ppermute x6, starting transfers between devices: 6.86 us -> 3.56 us  [from_partner(): return lax.ppermute(block, axis, route)]
  transfers between devices with their start and end apart: 9 -> 23, of which waited for: 7 -> 6; matrix products, arithmetic and copies ran while one was open for 9% -> 12% of each run, Pallas kernels for 0% -> 0%
where the time goes in v1:
time: 293 us
  waiting for transfers between devices  213 us (73%)
  starting transfers between devices  28.2 us (10%)
  local copies, waits for them, and re-layouts  27 us (9%)
  other arithmetic  10.7 us (4%)
  matrix products  10.7 us (4%)
  loops' own time  3.46 us (1%)
    ppermute x2, waiting for transfers between devices, passed_along(): lax.ppermute(array, axis, [(i, (i + by) % length) for i in range(length)])  135 us
    ppermute x15, waiting for transfers between devices, regions_expand(): jax.lax.ppermute(n_now, across, [(m, m ^ dev_j) for m in range(parts_out)])  47.3 us
    ppermute x6, waiting for transfers between devices, from_partner(): return lax.ppermute(block, axis, route)  29.9 us
    ppermute x15, starting transfers between devices, regions_expand(): jax.lax.ppermute(n_now, across, [(m, m ^ dev_j) for m in range(parts_out)])  21.7 us
    unnamed x34, local copies, waits for them, and re-layouts  11.7 us
    select_n x3, other arithmetic, shards(): jnp.where(upper_half, jnp.concatenate([partner, features], 1), jnp.concat...  7.86 us
    dot_general x4, matrix products, add_columns(): jnp.dot(columns, block_piece, preferred_element_type=jnp.float32)  5.98 us
  transfers between devices with their start and end apart: 23, of which 6 were waited for; matrix products, arithmetic and copies ran while one was open for 12% of the time, Pallas kernels for 0%

profile of v1, /device:TPU:0, one launch (start us, length us, event | category | flops | bytes accessed | tf_op | source)
XLA Modules:
  0.0 292.7 jit_solution(7524180392895516464)
XLA Ops:
  0.0 1.9 dynamic-slice_bitcast_fusion
  2.4 2.6 collective-permute-start.9
  5.1 1.8 collective-permute-start.11
  7.9 2.6 slice_bitcast_fusion.2
  10.5 3.1 %maximum_select_fusion.2 = bf16[512,1280]{1,0:T(8,128)(2,1)} fusion(bf16[512,640]{1,0:T(8,128)(2,1)} %bitcast.101, bf16[512,640]{1,0:T(8,128)(2,1)} %collective-permute-done, pred[]{:T(512)S(6)} %eq.65), kind=kLoop, calls=%fused_computation.26 | loop fusion | flops 5898240 | bytes 2621441 | tf_op jit(solution)/shard_map/jit(_where)/select_n | solution.py:70
  13.6 1.5 collective-permute-start.1
  15.1 2.0 slice_bitcast_fusion.1
  18.4 1.4 bitcast_dynamic-update-slice_fusion.14
  19.7 1.5 collective-permute-start.13
  21.3 1.4 bitcast_dynamic-update-slice_fusion.13
  22.6 23.3 %collective-permute-done.1 = bf16[512,1280]{1,0:T(8,128)(2,1)} collective-permute-done((bf16[512,1280]{1,0:T(8,128)(2,1)}, bf16[512,1280]{1,0:T(8,128)(2,1)}, u32[]{:S(2)}, u32[]{:S(2)}) %collective-permute-start.1) | collective-permute-done | bytes 1310752 | tf_op jit(solution)/shard_map/ppermute | solution.py:45
  46.7 3.2 %maximum_select_fusion.1 = bf16[512,2560]{1,0:T(8,128)(2,1)S(1)} fusion(bf16[512,1280]{1,0:T(8,128)(2,1)} %maximum_select_fusion.2, bf16[512,1280]{1,0:T(8,128)(2,1)} %collective-permute-done.1, pred[]{:T(512)S(6)} %eq.64), kind=kLoop, calls=%fused_computation.20 | loop fusion | flops 11796480 | bytes 5242881 | tf_op jit(solution)/shard_map/jit(_where)/select_n | solution.py:70
  49.9 1.6 collective-permute-start.2
  51.5 1.4 bitcast_dynamic-update-slice_fusion.12
  52.9 2.6 collective-permute-start.15
  55.5 1.4 bitcast_dynamic-update-slice_fusion.11
  57.8 2.5 collective-permute-start.17
  62.4 47.3 %collective-permute-done.15 = bf16[1,2,16,640]{3,2,1,0:T(8,128)(2,1)S(1)} collective-permute-done((bf16[1,2,16,640]{3,2,1,0:T(8,128)(2,1)S(1)}, bf16[1,2,16,640]{3,2,1,0:T(8,128)(2,1)S(1)}, u32[]{:S(2)}, u32[]{:S(2)}) %collective-permute-start.15) | collective-permute-done | bytes 40992 | tf_op jit(solution)/shard_map/ppermute | solution.py:32
  109.7 2.5 collective-permute-start.19
  113.9 2.1 collective-permute-start.21
  116.7 2.8 collective-permute-start.22
  120.8 2.9 collective-permute-start.4
  124.9 1.6 maximum_select_fusion
  126.5 1.2 fusion.20
  127.7 101.5 %collective-permute-done.3 = bf16[1280,640]{1,0:T(8,128)(2,1)S(1)} collective-permute-done((bf16[1280,640]{1,0:T(8,128)(2,1)S(1)}, bf16[1280,640]{1,0:T(8,128)(2,1)S(1)}, u32[]{:S(2)}, u32[]{:S(2)}) %collective-permute-start.3) | collective-permute-done | bytes 1638432 | tf_op jit(solution)/shard_map/while/body/eval_jaxpr/ppermute | solution.py:50
  230.4 33.8 %collective-permute-done.4 = bf16[1280,640]{1,0:T(8,128)(2,1)S(1)} collective-permute-done((bf16[1280,640]{1,0:T(8,128)(2,1)S(1)}, bf16[1280,640]{1,0:T(8,128)(2,1)S(1)}, u32[]{:S(2)}, u32[]{:S(2)}) %collective-permute-start.4) | collective-permute-done | bytes 1638432 | tf_op jit(solution)/shard_map/while/body/eval_jaxpr/ppermute | solution.py:50
  264.2 1.2 fusion.16
  265.4 2.3 multiply_reduce_fusion
  268.4 1.7 gather_fusion
  270.6 3.3 %collective-permute-done.6 = f32[512]{0:T(512)S(1)} collective-permute-done((f32[512]{0:T(512)S(1)}, f32[512]{0:T(512)S(1)}, u32[]{:S(2)}, u32[]{:S(2)}) %collective-permute-start.6) | collective-permute-done | bytes 2080 | tf_op jit(solution)/shard_map/ppermute | solution.py:45
  274.1 3.4 %collective-permute-done.7 = f32[512]{0:T(512)S(1)} collective-permute-done((f32[512]{0:T(512)S(1)}, f32[512]{0:T(512)S(1)}, u32[]{:S(2)}, u32[]{:S(2)}) %collective-permute-start.7) | collective-permute-done | bytes 2080 | tf_op jit(solution)/shard_map/ppermute | solution.py:45
  277.7 14.0 %while.2 = (s32[]{:T(128)}, bf16[5,512,128]{1,2,0:T(8,128)(2,1)S(1)}, pred[768]{0:T(1024)(128)(4,1)S(1)}, s32[5]{0:T(128)S(1)}, bf16[512,640]{1,0:T(8,128)(2,1)S...) while((s32[]{:T(128)}, ...), condition=%wide.region_6.7_spmd, body=%wide.region_3.6_spmd.sunk | while | flops 204995584 | bytes 5912495 | solution.py:138
  (111 shorter events, 25.6 us)
Async XLA Ops:
  0.0 7.7 %copy-start = (s32[2,16]{1,0:T(2,128)S(1)}, s32[2,16]{1,0:T(2,128)}, u32[]{:S(2)}) copy-start(s32[2,16]{1,0:T(2,128)} %param.15) | copy-start | bytes 388
  1.9 16.2 %collective-permute-start.8 = (bf16[1,2,16,640]{3,2,1,0:T(8,128)(2,1)}, bf16[1,2,16,640]{3,2,1,0:T(8,128)(2,1)}, u32[]{:S(2)}, u32[]{:S(2)}) collective-permute-start(bf16[1,2,16,640]{3,2,1,0:T(8,128)(2,1)} %get-tuple-element.100), channel_id=1, source_target_pairs={{0,1},{1,0},{2,3},{3,2},{4,5},{5,4},{6,7},{7,6},{8,9},{9,8},{10,11... | collective-permute-start | bytes 122888 | tf_op jit(solution)/shard_map/ppermute | solution.py:32
  2.4 17.3 %collective-permute-start.9 = (bf16[1,2,16,640]{3,2,1,0:T(8,128)(2,1)}, bf16[1,2,16,640]{3,2,1,0:T(8,128)(2,1)}, u32[]{:S(2)}, u32[]{:S(2)}) collective-permute-start(bf16[1,2,16,640]{3,2,1,0:T(8,128)(2,1)} %get-tuple-element.99), channel_id=1, source_target_pairs={{0,2},{1,3},{2,0},{3,1},{4,6},{5,7},{6,4},{7,5},{8,10},{9,11},{10,... | collective-permute-start | bytes 122888 | tf_op jit(solution)/shard_map/ppermute | solution.py:32
  5.0 44.9 %collective-permute-start.10 = (bf16[1,2,16,640]{3,2,1,0:T(8,128)(2,1)}, bf16[1,2,16,640]{3,2,1,0:T(8,128)(2,1)}, u32[]{:S(2)}, u32[]{:S(2)}) collective-permute-start(bf16[1,2,16,640]{3,2,1,0:T(8,128)(2,1)} %get-tuple-element.98), channel_id=1, source_target_pairs={{0,3},{1,2},{2,1},{3,0},{4,7},{5,6},{6,5},{7,4},{8,11},{9,10},{10,... | collective-permute-start | bytes 122888 | tf_op jit(solution)/shard_map/ppermute | solution.py:32
  5.1 47.8 %collective-permute-start.11 = (bf16[1,2,16,640]{3,2,1,0:T(8,128)(2,1)}, bf16[1,2,16,640]{3,2,1,0:T(8,128)(2,1)}, u32[]{:S(2)}, u32[]{:S(2)}) collective-permute-start(bf16[1,2,16,640]{3,2,1,0:T(8,128)(2,1)} %get-tuple-element.97), channel_id=1, source_target_pairs={{0,4},{1,5},{2,6},{3,7},{4,0},{5,1},{6,2},{7,3},{8,12},{9,13},{10,... | collective-permute-start | bytes 122888 | tf_op jit(solution)/shard_map/ppermute | solution.py:32
  6.9 3.7 %collective-permute-start = (bf16[512,640]{1,0:T(8,128)(2,1)}, bf16[512,640]{1,0:T(8,128)(2,1)}, u32[]{:S(2)}, u32[]{:S(2)}) collective-permute-start(bf16[512,640]{1,0:T(8,128)(2,1)} %bitcast.100), channel_id=1, source_target_pairs={{0,1},{1,0},{2,3},{3,2},{4,5},{5,4},{6,7},{7,6},{8,9},{9,8},{10,11... | collective-permute-start | bytes 1966088 | tf_op jit(solution)/shard_map/ppermute | solution.py:45
  7.9 7.2 %copy-start.1 = (bf16[1,2560,640]{2,1,0:T(8,128)(2,1)S(1)}, bf16[1,2560,640]{2,1,0:T(8,128)(2,1)}, u32[]{:S(2)}) copy-start(bf16[1,2560,640]{2,1,0:T(8,128)(2,1)} %param.10) | copy-start | bytes 9830404
  13.6 32.3 %collective-permute-start.1 = (bf16[512,1280]{1,0:T(8,128)(2,1)}, bf16[512,1280]{1,0:T(8,128)(2,1)}, u32[]{:S(2)}, u32[]{:S(2)}) collective-permute-start(bf16[512,1280]{1,0:T(8,128)(2,1)} %maximum_select_fusion.2), channel_id=1, source_target_pairs={{0,2},{2,0},{1,3},{3,1},{4,6},{6,4},{5,7},{7,5},{8,10},{10,8},{9,1... | collective-permute-start | bytes 3932168 | tf_op jit(solution)/shard_map/ppermute | solution.py:45
  18.1 38.8 %collective-permute-start.12 = (bf16[1,2,16,640]{3,2,1,0:T(8,128)(2,1)}, bf16[1,2,16,640]{3,2,1,0:T(8,128)(2,1)S(1)}, u32[]{:S(2)}, u32[]{:S(2)}) collective-permute-start(bf16[1,2,16,640]{3,2,1,0:T(8,128)(2,1)} %get-tuple-element.96), channel_id=1, source_target_pairs={{0,5},{1,4},{2,7},{3,6},{4,1},{5,0},{6,3},{7,2},{8,13},{9,12},{10,... | collective-permute-start | bytes 122888 | tf_op jit(solution)/shard_map/ppermute | solution.py:32
  19.7 38.0 %collective-permute-start.13 = (bf16[1,2,16,640]{3,2,1,0:T(8,128)(2,1)}, bf16[1,2,16,640]{3,2,1,0:T(8,128)(2,1)S(1)}, u32[]{:S(2)}, u32[]{:S(2)}) collective-permute-start(bf16[1,2,16,640]{3,2,1,0:T(8,128)(2,1)} %get-tuple-element.95), channel_id=1, source_target_pairs={{0,6},{1,7},{2,4},{3,5},{4,2},{5,3},{6,0},{7,1},{8,14},{9,15},{10,... | collective-permute-start | bytes 122888 | tf_op jit(solution)/shard_map/ppermute | solution.py:32
  45.9 7.0 %copy-start.9 = (bf16[1,2,16,640]{3,2,1,0:T(8,128)(2,1)S(1)}, bf16[1,2,16,640]{3,2,1,0:T(8,128)(2,1)}, u32[]{:S(2)}) copy-start(bf16[1,2,16,640]{3,2,1,0:T(8,128)(2,1)} %get-tuple-element.93) | copy-start | bytes 122884
  45.9 11.0 %copy-start.8 = (bf16[1,2,16,640]{3,2,1,0:T(8,128)(2,1)S(1)}, bf16[1,2,16,640]{3,2,1,0:T(8,128)(2,1)}, u32[]{:S(2)}) copy-start(bf16[1,2,16,640]{3,2,1,0:T(8,128)(2,1)} %get-tuple-element.92) | copy-start | bytes 122884
  45.9 74.2 %copy-start.6 = (bf16[1280,640]{1,0:T(8,128)(2,1)S(1)}, bf16[1280,640]{1,0:T(8,128)(2,1)}, u32[]{:S(2)}) copy-start(bf16[1280,640]{1,0:T(8,128)(2,1)} %get-tuple-element.80) | copy-start | bytes 4915204
  45.9 74.8 %copy-start.5 = (bf16[1280,640]{1,0:T(8,128)(2,1)S(1)}, bf16[1280,640]{1,0:T(8,128)(2,1)}, u32[]{:S(2)}) copy-start(bf16[1280,640]{1,0:T(8,128)(2,1)} %get-tuple-element.81) | copy-start | bytes 4915204
  45.9 15.0 %collective-permute-start.14 = (bf16[1,2,16,640]{3,2,1,0:T(8,128)(2,1)}, bf16[1,2,16,640]{3,2,1,0:T(8,128)(2,1)S(1)}, u32[]{:S(2)}, u32[]{:S(2)}) collective-permute-start(bf16[1,2,16,640]{3,2,1,0:T(8,128)(2,1)} %get-tuple-element.94), channel_id=1, source_target_pairs={{0,7},{1,6},{2,5},{3,4},{4,3},{5,2},{6,1},{7,0},{8,15},{9,14},{10,... | collective-permute-start | bytes 122888 | tf_op jit(solution)/shard_map/ppermute | solution.py:32
  49.9 75.0 %collective-permute-start.2 = (bf16[512,2560]{1,0:T(8,128)(2,1)S(1)}, bf16[512,2560]{1,0:T(8,128)(2,1)S(1)}, u32[]{:S(2)}, u32[]{:S(2)}) collective-permute-start(bf16[512,2560]{1,0:T(8,128)(2,1)S(1)} %maximum_select_fusion.1), channel_id=1, source_target_pairs={{0,4},{4,0},{1,5},{5,1},{2,6},{6,2},{3,7},{7,3},{8,12},{12,8},{9,1... | collective-permute-start | bytes 7864328 | tf_op jit(solution)/shard_map/ppermute | solution.py:45
  52.9 56.7 %collective-permute-start.15 = (bf16[1,2,16,640]{3,2,1,0:T(8,128)(2,1)S(1)}, bf16[1,2,16,640]{3,2,1,0:T(8,128)(2,1)S(1)}, u32[]{:S(2)}, u32[]{:S(2)}) collective-permute-start(bf16[1,2,16,640]{3,2,1,0:T(8,128)(2,1)S(1)} %copy-done.9), channel_id=1, source_target_pairs={{0,8},{1,9},{2,10},{3,11},{4,12},{5,13},{6,14},{7,15},{8,0},{9,1},... | collective-permute-start | bytes 122888 | tf_op jit(solution)/shard_map/ppermute | solution.py:32
  56.9 55.9 %collective-permute-start.16 = (bf16[1,2,16,640]{3,2,1,0:T(8,128)(2,1)S(1)}, bf16[1,2,16,640]{3,2,1,0:T(8,128)(2,1)S(1)}, u32[]{:S(2)}, u32[]{:S(2)}) collective-permute-start(bf16[1,2,16,640]{3,2,1,0:T(8,128)(2,1)S(1)} %copy-done.8), channel_id=1, source_target_pairs={{0,9},{1,8},{2,11},{3,10},{4,13},{5,12},{6,15},{7,14},{8,1},{9,0},... | collective-permute-start | bytes 122888 | tf_op jit(solution)/shard_map/ppermute | solution.py:32
  57.8 56.2 %collective-permute-start.17 = (bf16[1,2,16,640]{3,2,1,0:T(8,128)(2,1)S(1)}, bf16[1,2,16,640]{3,2,1,0:T(8,128)(2,1)S(1)}, u32[]{:S(2)}, u32[]{:S(2)}) collective-permute-start(bf16[1,2,16,640]{3,2,1,0:T(8,128)(2,1)S(1)} %get-tuple-element.91), channel_id=1, source_target_pairs={{0,10},{1,11},{2,8},{3,9},{4,14},{5,15},{6,12},{7,13},{8,2},{9,3},... | collective-permute-start | bytes 122888 | tf_op jit(solution)/shard_map/ppermute | solution.py:32
  60.9 55.8 %collective-permute-start.18 = (bf16[1,2,16,640]{3,2,1,0:T(8,128)(2,1)S(1)}, bf16[1,2,16,640]{3,2,1,0:T(8,128)(2,1)S(1)}, u32[]{:S(2)}, u32[]{:S(2)}) collective-permute-start(bf16[1,2,16,640]{3,2,1,0:T(8,128)(2,1)S(1)} %get-tuple-element.90), channel_id=1, source_target_pairs={{0,11},{1,10},{2,9},{3,8},{4,15},{5,14},{6,13},{7,12},{8,3},{9,2},... | collective-permute-start | bytes 122888 | tf_op jit(solution)/shard_map/ppermute | solution.py:32
  109.7 10.5 %collective-permute-start.19 = (bf16[1,2,16,640]{3,2,1,0:T(8,128)(2,1)S(1)}, bf16[1,2,16,640]{3,2,1,0:T(8,128)(2,1)S(1)}, u32[]{:S(2)}, u32[]{:S(2)}) collective-permute-start(bf16[1,2,16,640]{3,2,1,0:T(8,128)(2,1)S(1)} %get-tuple-element.89), channel_id=1, source_target_pairs={{0,12},{1,13},{2,14},{3,15},{4,8},{5,9},{6,10},{7,11},{8,4},{9,5},... | collective-permute-start | bytes 122888 | tf_op jit(solution)/shard_map/ppermute | solution.py:32
  112.8 8.0 %collective-permute-start.20 = (bf16[1,2,16,640]{3,2,1,0:T(8,128)(2,1)S(1)}, bf16[1,2,16,640]{3,2,1,0:T(8,128)(2,1)S(1)}, u32[]{:S(2)}, u32[]{:S(2)}) collective-permute-start(bf16[1,2,16,640]{3,2,1,0:T(8,128)(2,1)S(1)} %get-tuple-element.88), channel_id=1, source_target_pairs={{0,13},{1,12},{2,15},{3,14},{4,9},{5,8},{6,11},{7,10},{8,5},{9,4},... | collective-permute-start | bytes 122888 | tf_op jit(solution)/shard_map/ppermute | solution.py:32
  113.9 10.4 %collective-permute-start.21 = (bf16[1,2,16,640]{3,2,1,0:T(8,128)(2,1)S(1)}, bf16[1,2,16,640]{3,2,1,0:T(8,128)(2,1)S(1)}, u32[]{:S(2)}, u32[]{:S(2)}) collective-permute-start(bf16[1,2,16,640]{3,2,1,0:T(8,128)(2,1)S(1)} %get-tuple-element.87), channel_id=1, source_target_pairs={{0,14},{1,15},{2,12},{3,13},{4,10},{5,11},{6,8},{7,9},{8,6},{9,7},... | collective-permute-start | bytes 122888 | tf_op jit(solution)/shard_map/ppermute | solution.py:32
  116.7 151.1 %collective-permute-start.22 = (bf16[1,2,16,640]{3,2,1,0:T(8,128)(2,1)S(1)}, bf16[1,2,16,640]{3,2,1,0:T(8,128)(2,1)S(1)}, u32[]{:S(2)}, u32[]{:S(2)}) collective-permute-start(bf16[1,2,16,640]{3,2,1,0:T(8,128)(2,1)S(1)} %get-tuple-element.86), channel_id=1, source_target_pairs={{0,15},{1,14},{2,13},{3,12},{4,11},{5,10},{6,9},{7,8},{8,7},{9,6},... | collective-permute-start | bytes 122888 | tf_op jit(solution)/shard_map/ppermute | solution.py:32
  120.1 109.1 %collective-permute-start.3 = (bf16[1280,640]{1,0:T(8,128)(2,1)S(1)}, bf16[1280,640]{1,0:T(8,128)(2,1)S(1)}, u32[]{:S(2)}, u32[]{:S(2)}) collective-permute-start(bf16[1280,640]{1,0:T(8,128)(2,1)S(1)} %copy-done.6), channel_id=1, source_target_pairs={{0,8},{1,9},{2,10},{3,11},{4,12},{5,13},{6,14},{7,15},{8,0},{9,1},... | collective-permute-start | bytes 4915208 | tf_op jit(solution)/shard_map/while/body/eval_jaxpr/ppermute | solution.py:50
  120.8 143.4 %collective-permute-start.4 = (bf16[1280,640]{1,0:T(8,128)(2,1)S(1)}, bf16[1280,640]{1,0:T(8,128)(2,1)S(1)}, u32[]{:S(2)}, u32[]{:S(2)}) collective-permute-start(bf16[1280,640]{1,0:T(8,128)(2,1)S(1)} %copy-done.5), channel_id=1, source_target_pairs={{0,8},{1,9},{2,10},{3,11},{4,12},{5,13},{6,14},{7,15},{8,0},{9,1},... | collective-permute-start | bytes 4915208 | tf_op jit(solution)/shard_map/while/body/eval_jaxpr/ppermute | solution.py:50
  267.8 6.1 %copy-start.3 = (bf16[512,640]{1,0:T(8,128)(2,1)S(1)}, bf16[512,640]{1,0:T(8,128)(2,1)}, u32[]{:S(2)}) copy-start(bf16[512,640]{1,0:T(8,128)(2,1)} %get-tuple-element.82) | copy-start | bytes 1966084
  267.8 6.1 %copy-start.4 = (bf16[512,640]{1,0:T(8,128)(2,1)S(1)}, bf16[512,640]{1,0:T(8,128)(2,1)}, u32[]{:S(2)}) copy-start(bf16[512,640]{1,0:T(8,128)(2,1)} %get-tuple-element.83) | copy-start | bytes 1966084
  267.8 2.4 collective-permute-start.5
  270.2 3.7 %collective-permute-start.6 = (f32[512]{0:T(512)S(1)}, f32[512]{0:T(512)S(1)}, u32[]{:S(2)}, u32[]{:S(2)}) collective-permute-start(f32[512]{0:T(512)S(1)} %add.172), channel_id=1, source_target_pairs={{0,2},{2,0},{1,3},{3,1},{4,6},{6,4},{5,7},{7,5},{8,10},{10,8},{9,1... | collective-permute-start | bytes 6152 | tf_op jit(solution)/shard_map/ppermute | solution.py:45
  273.9 3.6 %collective-permute-start.7 = (f32[512]{0:T(512)S(1)}, f32[512]{0:T(512)S(1)}, u32[]{:S(2)}, u32[]{:S(2)}) collective-permute-start(f32[512]{0:T(512)S(1)} %add.173), channel_id=1, source_target_pairs={{0,4},{4,0},{1,5},{5,1},{2,6},{6,2},{3,7},{7,3},{8,12},{12,8},{9,1... | collective-permute-start | bytes 6152 | tf_op jit(solution)/shard_map/ppermute | solution.py:45
  274.1 3.6 %copy-start.7 = (bf16[5,512,128]{1,2,0:T(8,128)(2,1)S(1)}, bf16[5,512,128]{1,2,0:T(8,128)(2,1)}, u32[]{:S(2)}) copy-start(bf16[5,512,128]{1,2,0:T(8,128)(2,1)} %custom-call.3) | copy-start | bytes 1966084
  (1 other events, 3.6 us)
